TPU v7x, 512 devices: a whole 4x4x16 slice. The times are simulated.
512 devices in a mesh: dp: 32 (over y, x, core), tensor: 16 (over z).
Axes of the slice: x: 4, y: 4, z: 16, core: 2. Of those that a mesh axis runs over, the one named last changes fastest.
Arguments:
- tokens: bfloat16 [16384, 8192], P('dp', 'tensor'), may hold values from -6 to 6
- row_adapter_index: int32 [16384, 1], P('dp'), may hold values from 0 to 255; in each aligned block of 512 rows (0 to 511, 512 to 1023, ...) at most 4 rows name the same one
- adapter_storage_slot: int32 [256], replicated, may hold values from 0 to 255, each once
- key_value_base_weight: bfloat16 [8192, 2, 1024], P('tensor'), may hold values from -0.09375 to 0.09375
- adapter_down_weight: bfloat16 [256, 8192, 128], P('dp', 'tensor'), may hold values from -0.0625 to 0.0625
- adapter_up_weight: bfloat16 [256, 2, 64, 1024], P('dp', None, None, 'tensor'), may hold values from -0.75 to 0.75
Outputs:
- key_value: bfloat16 [16384, 2, 1024], P('dp', None, 'tensor')
Inputs may be any that keep to these rules, and one draw needn't show every extreme that they name: `row_adapter_index`: within the rows of one index of dp no adapter is named by more than 4 rows, a bound that some block reaches. `adapter_storage_slot`: A permutation of the slots.
All inputs are finite; a program needn't handle non-finite values.
Results may differ from a plain program's by a relative error of at most 0.0034.
Values may be sent and summed in bfloat16 or wider, within the bound.
A program may use at most 64 MiB of HBM per device.

v0:
```python
import jax
import jax.numpy as jnp
from jax import lax
from jax.sharding import PartitionSpec as P

adapter_scale = 0.5


def per_device(
    tokens,
    row_adapter_index,
    adapter_storage_slot,
    key_value_base_weight,
    adapter_down_weight,
    adapter_up_weight,
):
    row_count, shard_width = tokens.shape
    local_adapter_slots = adapter_down_weight.shape[0]
    groups = lax.axis_size("dp")
    experts = local_adapter_slots * groups
    capacity = max(2, 2 * row_count // experts)
    doubled_rank = adapter_down_weight.shape[2]
    adapter_of = row_adapter_index[:, 0]
    columns = lax.broadcasted_iota(jnp.int32, (row_count, experts), 1)
    onehot = (adapter_of[:, None] == columns).astype(jnp.int32)
    earlier = jnp.cumsum(onehot, axis=0) - onehot
    position = jnp.sum(earlier * onehot, axis=1)
    storage_device = jnp.sum(onehot * adapter_storage_slot[None, :], axis=1)
    target = storage_device * capacity + position
    outbox = jnp.zeros((experts * capacity, shard_width), tokens.dtype).at[target].set(tokens)
    outbox = outbox.reshape(groups, local_adapter_slots, capacity, shard_width)
    partials = jnp.einsum(
        "rd,djn->rjn", tokens, key_value_base_weight, preferred_element_type=jnp.float32
    )
    base = lax.psum_scatter(partials, "tensor", scatter_dimension=2, tiled=True)
    pieces_sum = jnp.einsum(
        "sekd,edr->sekr",
        lax.all_to_all(outbox, "dp", split_axis=0, concat_axis=0, tiled=True),
        adapter_down_weight,
        preferred_element_type=jnp.float32,
    )
    reduced_rows = lax.psum(pieces_sum, "tensor").astype(jnp.bfloat16)
    dims_now = reduced_rows.shape
    reduced_rows = reduced_rows.reshape(dims_now[0], dims_now[1], dims_now[2], 2, doubled_rank // 2)
    adapter_delta = jnp.einsum(
        "upgtl,ptlz->upgtz", reduced_rows, adapter_up_weight, preferred_element_type=jnp.float32
    )
    adapter_delta = (adapter_scale * adapter_delta).astype(jnp.bfloat16)
    returned = lax.all_to_all(adapter_delta, "dp", split_axis=0, concat_axis=0, tiled=True)
    returned_flat = returned.reshape(experts * capacity, 2, returned.shape[-1])
    update_rows = returned_flat[target]
    return (base + update_rows.astype(jnp.float32)).astype(jnp.bfloat16)


def solution(mesh):
    placed = (
        P("dp", "tensor"),
        P("dp", None),
        P(),
        P("tensor", None, None),
        P("dp", "tensor", None),
        P("dp", None, None, "tensor"),
    )
    return jax.shard_map(
        per_device, mesh=mesh, in_specs=placed, out_specs=P("dp", None, "tensor"), check_vma=False
    )
```

profile of v0, /device:TPU:1, one launch (start us, length us, event | category | flops | bytes accessed | tf_op | source)
XLA Modules:
  0.0 144.0 jit_solution(11326901580064575148)
XLA Ops:
  6.5 0.0 copy-start
  6.5 0.0 reduce-scatter.2.cloned.1.call-start
  6.5 1.6 %copy-done = bf16[512,2,1024]{2,1,0:T(2,128)(2,1)S(1)} copy-done((bf16[512,2,1024]{2,1,0:T(2,128)(2,1)S(1)}, bf16[512,2,1024]{2,1,0:T(2,128)(2,1)}, u32[]{:S(2)}) %copy-start) | copy-done | bytes 2097176
  8.1 4.3 %fusion = f32[512,2,1024]{0,2,1:T(8,128)} fusion(bf16[512,2,1024]{2,1,0:T(2,128)(2,1)S(1)} %copy-done, bf16[512,512]{1,0:T(8,128)(2,1)} %param.6), kind=kOutput, calls=%fused_computation.2 | convolution fusion | flops 1073741824 | bytes 6815744 | tf_op jit(solution)/shard_map/rd,djn->rjn/dot_general | solution.py:32
  12.4 0.0 copy-start.2
  12.4 0.0 reduce-scatter.2.cloned.1.call-update
  12.5 0.0 copy-start.3
  12.5 0.6 copy-done.2
  13.1 0.1 copy.19
  13.2 0.2 fusion.10
  13.5 0.1 copy.20
  13.6 0.0 copy-done.3
  13.7 0.4 select_reduce_fusion
  14.0 3.2 %scatter_custom_fusion = bf16[1024,512]{1,0:T(8,128)(2,1)S(1)} fusion(s32[512]{0:T(512)S(1)} %bitcast.51, bf16[512,512]{1,0:T(8,128)(2,1)} %param.6, bf16[]{:T(256)} %constant.5.clone.1), kind=kCustom, calls=%fused_computation.20 | custom fusion | bytes 1049088 | tf_op jit(solution)/shard_map/scatter | solution.py:30
  17.3 1.1 reshape.51
  18.4 0.0 copy-start.1
  18.4 27.9 %all_to_all.10 = bf16[32,8,4,512]{3,2,1,0:T(4,128)(2,1)S(1)} all-to-all(bf16[32,8,4,512]{3,2,1,0:T(4,128)(2,1)} %reshape.51), channel_id=1, replica_groups=mesh['dp'=32,'tensor'=16] {'dp'}, dimensions={0} | all-to-all | bytes 2097152 | tf_op jit(solution)/shard_map/all_to_all | solution.py:38
  46.3 0.0 copy-done.1
  46.3 0.0 copy-start.4
  46.3 0.8 convolution_bitcast_fusion
  47.1 61.2 %all-reduce.1 = bf16[32,8,4,128]{3,0,2,1:T(8,128)(2,1)S(1)} all-reduce(f32[32,8,4,128]{3,0,2,1:T(8,128)S(1)} %convolution_bitcast_fusion), channel_id=1, replica_groups=mesh['dp'=32,'tensor'=16] {'tensor'}, use_global_device_ids=true, to_apply=%region_6.7 | all-reduce | flops 131072 | bytes 786432 | tf_op jit(solution)/shard_map/psum | solution.py:42
  108.3 0.2 reshape.52
  108.5 0.0 copy-done.4
  108.5 0.3 fusion.3
  108.8 0.3 copy.36
  109.1 1.1 reshape.75
  110.2 13.0 %all-to-all-start.1 = ((bf16[32,2,2048]{2,1,0:T(2,128)(2,1)}), bf16[32,2,2048]{2,1,0:T(2,128)(2,1)S(1)}, u32[]{:S(2)}, u32[]{:S(2)}) async-start(bf16[32,2,2048]{2,1,0:T(2,128)(2,1)} %reshape.75), calls=%async_computation.2 | async-start | bytes 524288 | tf_op jit(solution)/shard_map/all_to_all | solution.py:49
  123.3 8.9 %all-to-all-done.1 = bf16[32,2,2048]{2,1,0:T(2,128)(2,1)S(1)} async-done(((bf16[32,2,2048]{2,1,0:T(2,128)(2,1)}), bf16[32,2,2048]{2,1,0:T(2,128)(2,1)S(1)}, u32[]{:S(2)}, u32[]{:S(2)}) %all-to-all-start.1) | async-done | bytes 262176 | tf_op jit(solution)/shard_map/all_to_all | solution.py:49
  132.1 0.4 reshape.76
  132.5 0.2 copy.24
  132.7 0.5 copy.25
  133.2 2.1 %gather_fusion = bf16[512,2,64]{2,1,0:T(2,128)(2,1)S(1)} fusion(bf16[1024,2,64]{2,1,0:T(2,128)(2,1)S(1)} %copy.25, s32[1024]{0:T(1024)S(1)} %pad_clamp_fusion), kind=kCustom, calls=%fused_computation | custom fusion | bytes 264192 | tf_op jit(solution)/shard_map/gather | solution.py:51
  135.4 0.1 copy.26
  135.5 0.0 reduce-scatter.2.cloned.1.call-done
  135.5 1.6 %add_convert_fusion = bf16[512,2,64]{0,2,1:T(8,128)(2,1)} fusion(f32[512,2,64]{0,2,1:T(8,128)} %reduce-scatter.2.cloned.1.call-done, bf16[512,2,64]{0,2,1:T(8,128)(2,1)S(1)} %copy.26), kind=kLoop, calls=%fused_computation.23 | loop fusion | flops 196608 | bytes 524288 | tf_op jit(solution)/shard_map/convert_element_type | solution.py:52
  (8 shorter events, 0.1 us)
Async XLA Ops:
  6.5 1.6 %copy-start = (bf16[512,2,1024]{2,1,0:T(2,128)(2,1)S(1)}, bf16[512,2,1024]{2,1,0:T(2,128)(2,1)}, u32[]{:S(2)}) copy-start(bf16[512,2,1024]{2,1,0:T(2,128)(2,1)} %param.9) | copy-start | bytes 6291460
  6.5 129.0 %reduce-scatter.2.cloned.1.call-start = ((), (), s32[]{:S(2)}) async-start(), calls=%async_computation.3 | async-start | bytes 4456448 | tf_op jit(solution)/shard_map/reduce_scatter | solution.py:35
  12.4 0.7 copy-start.2
  12.5 1.2 copy-start.3
  18.4 27.9 %copy-start.1 = (bf16[8,512,128]{2,1,0:T(8,128)(2,1)S(1)}, bf16[8,512,128]{2,1,0:T(8,128)(2,1)}, u32[]{:S(2)}) copy-start(bf16[8,512,128]{2,1,0:T(8,128)(2,1)} %param.10) | copy-start | bytes 3145732
  46.3 62.3 %copy-start.4 = (bf16[8,2,64,64]{3,2,1,0:T(8,128)(2,1)S(1)}, bf16[8,2,64,64]{3,2,1,0:T(8,128)(2,1)}, u32[]{:S(2)}) copy-start(bf16[8,2,64,64]{3,2,1,0:T(8,128)(2,1)} %param.11) | copy-start | bytes 393220
  110.2 22.0 %all-to-all-start.1 = ((bf16[32,2,2048]{2,1,0:T(2,128)(2,1)}), bf16[32,2,2048]{2,1,0:T(2,128)(2,1)S(1)}, u32[]{:S(2)}, u32[]{:S(2)}) async-start(bf16[32,2,2048]{2,1,0:T(2,128)(2,1)} %reshape.75), calls=%async_computation.2 | async-start | bytes 524288 | tf_op jit(solution)/shard_map/all_to_all | solution.py:49
Sparse Core Ops, SparseCore 0:
  12.6 79.6 reduce-scatter.1
where the time goes:
time: 144 us
  blocking collectives  89.1 us (62%)
  between operations  13.6 us (9%)
  starting transfers between devices  13 us (9%)
  local copies, waits for them, and re-layouts  11.8 us (8%)
  waiting for transfers between devices  8.92 us (6%)
  matrix products  5.38 us (4%)
  other arithmetic  2.28 us (2%)
    psum x1, blocking collectives, per_device(): reduced_rows = lax.psum(pieces_sum, 'tensor').astype(jnp.bfloat16)  61.2 us
    all_to_all x1, blocking collectives, per_device(): lax.all_to_all(outbox, 'dp', split_axis=0, concat_axis=0, tiled=True)  27.9 us
    all_to_all x1, starting transfers between devices, per_device(): lax.all_to_all(adapter_delta, 'dp', split_axis=0, concat_axis=0, tiled=True)  13 us
    all_to_all x1, waiting for transfers between devices, per_device(): lax.all_to_all(adapter_delta, 'dp', split_axis=0, concat_axis=0, tiled=True)  8.89 us
    dot_general x1, matrix products, per_device(): jnp.einsum('rd,djn->rjn', tokens, key_value_base_weight, preferred_elemen...  4.31 us
    unnamed x13, local copies, waits for them, and re-layouts  3.69 us
    scatter x1, local copies, waits for them, and re-layouts, per_device(): jnp.zeros((experts * capacity, shard_width), tokens.dtype).at[target]  3.22 us
  transfers between devices with their start and end apart: 2, of which 1 were waited for; matrix products, arithmetic and copies ran while one was open for 8% of the time, Pallas kernels for 0%

commit v1 on v0

--- a/solution.py
+++ b/solution.py
@@ -4,6 +4,12 @@
 from jax.sharding import PartitionSpec as P
 
 adapter_scale = 0.5
+
+
+def summed_here(x, axis):
+    parts = lax.all_gather(x, axis, axis=0, tiled=False)
+    total = parts.sum(axis=0)
+    return total
 
 
 def per_device(
@@ -39,7 +45,7 @@
         adapter_down_weight,
         preferred_element_type=jnp.float32,
     )
-    reduced_rows = lax.psum(pieces_sum, "tensor").astype(jnp.bfloat16)
+    reduced_rows = summed_here(pieces_sum, "tensor").astype(jnp.bfloat16)
     dims_now = reduced_rows.shape
     reduced_rows = reduced_rows.reshape(dims_now[0], dims_now[1], dims_now[2], 2, doubled_rank // 2)
     adapter_delta = jnp.einsum(

time: 144 us -> 236 us (1.64)
  the two profiles are of different devices: /device:TPU:1 before, /device:TPU:4 now
where the time goes in v1:
time: 236 us; the launch traced here: 235 us
  waiting for transfers between devices  167 us (71%)
  blocking collectives  25 us (11%)
  between operations  13.6 us (6%)
  local copies, waits for them, and re-layouts  10.4 us (4%)
  starting transfers between devices  7.45 us (3%)
  other arithmetic  6.77 us (3%)
  matrix products  5.22 us (2%)
    all_gather x1, waiting for transfers between devices, summed_here(): parts = lax.all_gather(x, axis, axis=0, tiled=False)  103 us
    reduce_scatter x1, waiting for transfers between devices, per_device(): base = lax.psum_scatter(partials, 'tensor', scatter_dimension=2, tiled=True)  56.8 us
    all_to_all x1, blocking collectives, per_device(): lax.all_to_all(outbox, 'dp', split_axis=0, concat_axis=0, tiled=True)  25 us
    all_to_all x1, starting transfers between devices, per_device(): lax.all_to_all(adapter_delta, 'dp', split_axis=0, concat_axis=0, tiled=True)  7.41 us
    all_to_all x1, waiting for transfers between devices, per_device(): lax.all_to_all(adapter_delta, 'dp', split_axis=0, concat_axis=0, tiled=True)  6.75 us
  transfers between devices with their start and end apart: 3, of which 3 were waited for; matrix products, arithmetic and copies ran while one was open for 6% of the time, Pallas kernels for 0%

profile of v1, /device:TPU:4, one launch (start us, length us, event | category | flops | bytes accessed | tf_op | source)
XLA Modules:
  0.0 235.2 jit_solution(1538117031680890654)
XLA Ops:
  6.5 0.0 copy-start
  6.5 0.0 copy-start.3
  6.5 0.0 copy-start.4
  6.5 0.0 all-gather.3.cloned.1.call-start
  6.5 0.9 copy.18
  7.5 0.2 fusion.10
  7.8 0.1 copy.19
  7.9 0.0 copy-done.3
  7.9 0.0 copy-done.4
  7.9 0.4 select_reduce_fusion
  8.3 3.2 %scatter_custom_fusion = bf16[1024,512]{1,0:T(8,128)(2,1)S(1)} fusion(s32[512]{0:T(512)S(1)} %bitcast.53, bf16[512,512]{1,0:T(8,128)(2,1)} %param.6, bf16[]{:T(256)} %constant.6.clone.1), kind=kCustom, calls=%fused_computation.20 | custom fusion | bytes 1049088 | tf_op jit(solution)/shard_map/scatter | solution.py:36
  11.5 1.1 reshape.51
  12.7 0.0 copy-start.1
  12.7 25.0 %all_to_all.10 = bf16[32,8,4,512]{3,2,1,0:T(4,128)(2,1)S(1)} all-to-all(bf16[32,8,4,512]{3,2,1,0:T(4,128)(2,1)} %reshape.51), channel_id=1, replica_groups=mesh['dp'=32,'tensor'=16] {'dp'}, dimensions={0} | all-to-all | bytes 2097152 | tf_op jit(solution)/shard_map/all_to_all | solution.py:44
  37.6 0.0 copy-done.1
  37.7 0.0 copy-start.2
  37.7 1.6 convolution_bitcast_fusion
  39.3 0.0 all-gather.3.cloned.1.call-update
  39.3 0.0 reduce-scatter.2.cloned.1.call-start
  39.4 0.0 copy-done
  39.4 0.0 copy-done.2
  39.4 3.3 %fusion = f32[512,2,1024]{0,2,1:T(8,128)} fusion(bf16[512,2,1024]{2,1,0:T(2,128)(2,1)S(1)} %copy-done, bf16[512,512]{1,0:T(8,128)(2,1)S(1)} %copy-done.2), kind=kOutput, calls=%fused_computation.2 | convolution fusion | flops 1073741824 | bytes 6815744 | tf_op jit(solution)/shard_map/rd,djn->rjn/dot_general | solution.py:38
  42.7 0.0 reduce-scatter.2.cloned.1.call-update
  42.7 103.2 %all-gather.3.cloned.1.call-done = f32[512,8,4,128]{3,0,2,1:T(8,128)} async-done(((f32[32,8,4,128]{3,0,2,1:T(8,128)}), f32[512,8,4,128]{3,0,2,1:T(8,128)}) %all-gather.3.cloned.1.call-update) | async-done | bytes 8388624 | tf_op jit(solution)/shard_map/all_gather | solution.py:10
  145.9 0.0 copy-start.5
  145.9 4.5 %reduce_sum.29 = bf16[32,8,4,128]{3,0,2,1:T(8,128)(2,1)S(1)} reduce(f32[16,32,8,4,128]{4,1,0,3,2:T(8,128)} %bitcast.44, f32[]{:T(128)} %constant.16.clone.1), dimensions={0}, to_apply=%region_6.7 | reduce | flops 1966080 | bytes 8650756 | tf_op jit(solution)/shard_map/reduce_sum | solution.py:11
  150.4 0.2 reshape.73
  150.7 0.0 copy-done.5
  150.7 0.3 fusion.3
  151.0 0.3 copy.38
  151.2 1.1 reshape.76
  152.3 7.4 %all-to-all-start.1 = ((bf16[32,2,2048]{2,1,0:T(2,128)(2,1)}), bf16[32,2,2048]{2,1,0:T(2,128)(2,1)S(1)}, u32[]{:S(2)}, u32[]{:S(2)}) async-start(bf16[32,2,2048]{2,1,0:T(2,128)(2,1)} %reshape.76), calls=%async_computation.2 | async-start | bytes 524288 | tf_op jit(solution)/shard_map/all_to_all | solution.py:55
  159.8 6.7 %all-to-all-done.1 = bf16[32,2,2048]{2,1,0:T(2,128)(2,1)S(1)} async-done(((bf16[32,2,2048]{2,1,0:T(2,128)(2,1)}), bf16[32,2,2048]{2,1,0:T(2,128)(2,1)S(1)}, u32[]{:S(2)}, u32[]{:S(2)}) %all-to-all-start.1) | async-done | bytes 262176 | tf_op jit(solution)/shard_map/all_to_all | solution.py:55
  166.5 0.4 reshape.77
  166.9 0.2 copy.24
  167.1 0.5 copy.25
  167.6 2.1 gather_fusion
  169.7 0.1 copy.26
  169.9 56.8 %reduce-scatter.2.cloned.1.call-done = f32[512,2,64]{0,2,1:T(8,128)} async-done(((f32[512,2,1024]{0,2,1:T(8,128)}), f32[512,2,64]{0,2,1:T(8,128)}) %reduce-scatter.2.cloned.1.call-update) | async-done | bytes 262160 | tf_op jit(solution)/shard_map/reduce_scatter | solution.py:41
  226.7 1.6 add_convert_fusion
  (8 shorter events, 0.1 us)
Async XLA Ops:
  6.5 32.8 %copy-start = (bf16[512,2,1024]{2,1,0:T(2,128)(2,1)S(1)}, bf16[512,2,1024]{2,1,0:T(2,128)(2,1)}, u32[]{:S(2)}) copy-start(bf16[512,2,1024]{2,1,0:T(2,128)(2,1)} %param.9) | copy-start | bytes 6291460
  6.5 1.4 copy-start.3
  6.5 1.4 copy-start.4
  6.5 139.4 %all-gather.3.cloned.1.call-start = ((), (), s32[]{:S(2)}) async-start(), calls=%async_computation.4 | async-start | bytes 8912896 | tf_op jit(solution)/shard_map/all_gather | solution.py:10
  12.7 25.0 %copy-start.1 = (bf16[8,512,128]{2,1,0:T(8,128)(2,1)S(1)}, bf16[8,512,128]{2,1,0:T(8,128)(2,1)}, u32[]{:S(2)}) copy-start(bf16[8,512,128]{2,1,0:T(8,128)(2,1)} %param.10) | copy-start | bytes 3145732
  37.7 1.7 copy-start.2
  39.3 187.4 %reduce-scatter.2.cloned.1.call-start = ((), (), s32[]{:S(2)}) async-start(), calls=%async_computation.3 | async-start | bytes 4456448 | tf_op jit(solution)/shard_map/reduce_scatter | solution.py:41
  145.9 4.7 %copy-start.5 = (bf16[8,2,64,64]{3,2,1,0:T(8,128)(2,1)S(1)}, bf16[8,2,64,64]{3,2,1,0:T(8,128)(2,1)}, u32[]{:S(2)}) copy-start(bf16[8,2,64,64]{3,2,1,0:T(8,128)(2,1)} %param.11) | copy-start | bytes 393220
  152.3 14.2 %all-to-all-start.1 = ((bf16[32,2,2048]{2,1,0:T(2,128)(2,1)}), bf16[32,2,2048]{2,1,0:T(2,128)(2,1)S(1)}, u32[]{:S(2)}, u32[]{:S(2)}) async-start(bf16[32,2,2048]{2,1,0:T(2,128)(2,1)} %reshape.76), calls=%async_computation.2 | async-start | bytes 524288 | tf_op jit(solution)/shard_map/all_to_all | solution.py:55
Sparse Core Ops, SparseCore 0:
  39.4 106.4 all-gather.2
  148.8 77.9 reduce-scatter.1
